TPU v7x, 512 devices: a whole 4x4x16 slice. The times are simulated.
512 devices in a mesh: dp: 16 (over y, z_hi), seq: 32 (over z_lo, x, core).
Axes of the slice: x: 4, y: 4, z: 16 (z_hi: 4, z_lo: 4; z = z_hi * 4 + z_lo), core: 2. Of those that a mesh axis runs over, the one named last changes fastest.
Arguments:
- tokens: bfloat16 [1024, 64, 1152], P(('dp', 'seq')), may hold values from -6 to 6
- spatial_qkv: bfloat16 [1024, 64, 1728], P(('dp', 'seq')), may hold values from -6 to 6
- wo_spatial: bfloat16 [576, 1152], replicated, may hold values from -0.25 to 0.25
- w_temporal: bfloat16 [1152, 1728], P(None, 'dp'), may hold values from -0.1875 to 0.1875
- wo_temporal: bfloat16 [576, 1152], replicated, may hold values from -0.25 to 0.25
- cotangent: bfloat16 [1024, 64, 1152], P(('dp', 'seq')), may hold values from -24 to 24
Outputs:
- block_out: bfloat16 [1024, 64, 1152], P(('dp', 'seq'))
- tokens_grad: bfloat16 [1024, 64, 1152], P(('dp', 'seq'))
- spatial_qkv_grad: bfloat16 [1024, 64, 1728], P(('dp', 'seq'))
- wo_spatial_grad: float32 [576, 1152], P('seq', 'dp')
- wo_temporal_grad: float32 [576, 1152], P('seq', 'dp')
All inputs are finite; a program needn't handle non-finite values.
Results may differ from a plain program's by a relative error of at most 0.038.
Values may be sent and summed in bfloat16 or wider, within the bound.
A program may use at most 64 MiB of HBM per device.

v0:
```python
import math
import jax
import jax.numpy as jnp
from jax import lax
from jax.sharding import PartitionSpec as P

DH = 72
FRAMES = 16


def split_three(packed):
    inner_width = packed.shape[-1] // 3
    return (
        packed[..., :inner_width],
        packed[..., inner_width : 2 * inner_width],
        packed[..., 2 * inner_width :],
    )


def head_view(matrix):
    batch_size, length, inner_width = matrix.shape
    return matrix.reshape(batch_size, length, inner_width // DH, DH)


def attention_weights_of(query_heads, key_heads):
    scores = jnp.einsum(
        "blhd,bmhd->bhlm", query_heads, key_heads, preferred_element_type=jnp.float32
    ) * (1.0 / math.sqrt(DH))
    return jax.nn.softmax(scores, axis=-1)


def attention(queries, key_rows, values):
    batch_size, length, inner_width = queries.shape
    weights_full = attention_weights_of(head_view(queries), head_view(key_rows))
    rounded = weights_full.astype(jnp.bfloat16)
    output = jnp.einsum(
        "bhlm,bmhd->blhd", rounded, head_view(values), preferred_element_type=jnp.float32
    )
    return output.reshape(batch_size, length, inner_width).astype(jnp.bfloat16)


def attention_grad(queries, key_rows, values, output_grad):
    batch_size, length, inner_width = queries.shape
    query_heads = head_view(queries)
    key_heads = head_view(key_rows)
    value_heads = head_view(values)
    grad_heads = head_view(output_grad)
    weights_full = attention_weights_of(query_heads, key_heads)
    rounded = weights_full.astype(jnp.bfloat16)
    value_grad = jnp.einsum(
        "bhlm,blhd->bmhd", rounded, grad_heads, preferred_element_type=jnp.float32
    )
    weight_grad = jnp.einsum(
        "blhd,bmhd->bhlm", grad_heads, value_heads, preferred_element_type=jnp.float32
    )
    centered = weight_grad - jnp.sum(weights_full * weight_grad, axis=-1, keepdims=True)
    score_grad = (weights_full * centered * (1.0 / math.sqrt(DH))).astype(jnp.bfloat16)
    query_grad = jnp.einsum(
        "bhlm,bmhd->blhd", score_grad, key_heads, preferred_element_type=jnp.float32
    )
    key_grad = jnp.einsum(
        "bhlm,blhd->bmhd", score_grad, query_heads, preferred_element_type=jnp.float32
    )
    joined = [
        part_grad.reshape(batch_size, length, inner_width)
        for part_grad in (query_grad, key_grad, value_grad)
    ]
    return jnp.concatenate(joined, axis=-1).astype(jnp.bfloat16)


def to_clips(matrix, clip_count):
    frame_total, patch_share, channels = matrix.shape
    grouped = matrix.reshape(clip_count, FRAMES, patch_share, channels).transpose(0, 2, 1, 3)
    return grouped.reshape(clip_count * patch_share, FRAMES, channels)


def from_clips(matrix, clip_count):
    batch_rows, frame_count, channels = matrix.shape
    patch_share = batch_rows // clip_count
    grouped = matrix.reshape(clip_count, patch_share, frame_count, channels).transpose(0, 2, 1, 3)
    return grouped.reshape(clip_count * frame_count, patch_share, channels)


def times_transposed(left, right):
    return lax.dot_general(
        left, right, (((1,), (1,)), ((), ())), preferred_element_type=jnp.float32
    )


def transposed_times(left, right):
    return lax.dot_general(
        left, right, (((0,), (0,)), ((), ())), preferred_element_type=jnp.float32
    )


def forward_project(hidden_rows, weight_shard):
    return jnp.dot(
        hidden_rows,
        lax.all_gather(weight_shard, "dp", axis=1, tiled=True),
        preferred_element_type=jnp.float32,
    )


def backward_project(grad_rows, weight_shard):
    return times_transposed(grad_rows, lax.all_gather(weight_shard, "dp", axis=1, tiled=True))


def shards(tokens, spatial_qkv, wo_spatial, w_temporal, wo_temporal, cotangent):
    frames_dev, patches, feature_width = tokens.shape
    row_total = frames_dev * patches
    seq_devices = lax.axis_size("seq")
    clip_count = frames_dev * seq_devices // FRAMES
    spatial_query, spatial_keys, spatial_values = split_three(spatial_qkv)
    spatial_out = attention(spatial_query, spatial_keys, spatial_values)
    spatial_rows = spatial_out.reshape(row_total, -1)
    hidden_rows = (
        tokens.reshape(row_total, feature_width).astype(jnp.float32)
        + jnp.dot(spatial_rows, wo_spatial, preferred_element_type=jnp.float32)
    ).astype(jnp.bfloat16)
    frame_qkv = (
        forward_project(hidden_rows, w_temporal)
        .astype(jnp.bfloat16)
        .reshape(frames_dev, patches, -1)
    )
    patch_qkv = lax.all_to_all(frame_qkv, "seq", split_axis=1, concat_axis=0, tiled=True)
    temporal_query, temporal_keys, temporal_values = split_three(to_clips(patch_qkv, clip_count))
    patch_out = from_clips(attention(temporal_query, temporal_keys, temporal_values), clip_count)
    temporal_out = lax.all_to_all(patch_out, "seq", split_axis=0, concat_axis=1, tiled=True)
    temporal_rows = temporal_out.reshape(row_total, -1)
    block_out = (
        hidden_rows.astype(jnp.float32)
        + jnp.dot(temporal_rows, wo_temporal, preferred_element_type=jnp.float32)
    ).astype(jnp.bfloat16)
    grad_rows = cotangent.reshape(row_total, feature_width)
    out_grad = (
        times_transposed(grad_rows, wo_temporal)
        .astype(jnp.bfloat16)
        .reshape(frames_dev, patches, -1)
    )
    temporal_part = transposed_times(temporal_rows, grad_rows).astype(jnp.bfloat16)
    patch_out_grad = lax.all_to_all(out_grad, "seq", split_axis=1, concat_axis=0, tiled=True)
    clip_qkv_grad = attention_grad(
        temporal_query, temporal_keys, temporal_values, to_clips(patch_out_grad, clip_count)
    )
    patch_qkv_grad = from_clips(clip_qkv_grad, clip_count)
    frame_qkv_grad = lax.all_to_all(patch_qkv_grad, "seq", split_axis=0, concat_axis=1, tiled=True)
    projection_grad = backward_project(frame_qkv_grad.reshape(row_total, -1), w_temporal).astype(
        jnp.bfloat16
    )
    tokens_grad = (grad_rows.astype(jnp.float32) + projection_grad.astype(jnp.float32)).astype(
        jnp.bfloat16
    )
    spatial_out_grad = (
        times_transposed(tokens_grad, wo_spatial)
        .astype(jnp.bfloat16)
        .reshape(frames_dev, patches, -1)
    )
    spatial_part = transposed_times(spatial_rows, tokens_grad).astype(jnp.bfloat16)
    spatial_qkv_grad = attention_grad(spatial_query, spatial_keys, spatial_values, spatial_out_grad)
    seq_sums = (
        lax.psum_scatter(spatial_part, "seq", scatter_dimension=0, tiled=True).astype(jnp.float32),
        lax.psum_scatter(temporal_part, "seq", scatter_dimension=0, tiled=True).astype(jnp.float32),
    )
    spatial_weight_grad, temporal_weight_grad = (
        lax.psum_scatter(
            seq_sums[0].astype(jnp.bfloat16), "dp", scatter_dimension=1, tiled=True
        ).astype(jnp.float32),
        lax.psum_scatter(
            seq_sums[1].astype(jnp.bfloat16), "dp", scatter_dimension=1, tiled=True
        ).astype(jnp.float32),
    )
    return (
        block_out.reshape(frames_dev, patches, feature_width),
        tokens_grad.reshape(frames_dev, patches, feature_width),
        spatial_qkv_grad,
        spatial_weight_grad,
        temporal_weight_grad,
    )


def solution(mesh):
    placed = (
        P(("dp", "seq"), None, None),
        P(("dp", "seq"), None, None),
        P(),
        P(None, "dp"),
        P(),
        P(("dp", "seq"), None, None),
    )
    return jax.shard_map(
        shards,
        mesh=mesh,
        in_specs=placed,
        out_specs=(
            P(("dp", "seq"), None, None),
            P(("dp", "seq"), None, None),
            P(("dp", "seq"), None, None),
            P("seq", "dp"),
            P("seq", "dp"),
        ),
        check_vma=False,
    )
```

profile of v0, /device:TPU:2, one launch (start us, length us, event | category | flops | bytes accessed | tf_op | source)
XLA Modules:
  0.0 741.1 jit_solution(11731465842137330203)
XLA Ops:
  7.2 0.7 all-gather.3.cloned.1.call-update
  7.9 0.6 copy-done
  8.5 1.5 convolution_convert_fusion.13
  10.2 0.8 copy.76
  11.0 10.1 %all-to-all-start.2 = ((bf16[2,64,576]{2,0,1:T(2,128)(2,1)}), bf16[2,64,576]{2,0,1:T(2,128)(2,1)}, u32[]{:S(2)}, u32[]{:S(2)}) async-start(bf16[2,64,576]{2,0,1:T(2,128)(2,1)} %copy.76), calls=%async_computation.2 | async-start | bytes 327680 | tf_op jit(solution)/shard_map/all_to_all | solution.py:141
  22.1 1.2 fusion.123
  23.3 2.4 fusion.21
  25.7 1.1 copy.62
  27.0 0.4 fusion.7
  27.4 121.9 %all-gather.3.cloned.1.call-done = bf16[16,108,1152]{2,1,0:T(8,128)(2,1)} async-done(((bf16[1,108,1152]{2,1,0:T(8,128)(2,1)}), bf16[16,108,1152]{2,1,0:T(8,128)(2,1)}) %all-gather.3.cloned.1.call-update) | async-done | bytes 3981328 | tf_op jit(solution)/shard_map/all_gather | solution.py:99
  149.4 4.8 reshape.139
  154.2 4.1 convolution_convert_fusion.3
  158.3 1.2 copy.63
  159.5 1.2 copy.64
  160.8 5.0 all-to-all-start
  165.7 1.0 copy.77
  166.8 0.7 copy.78
  167.5 1.9 reshape_reshape.6
  169.4 9.7 %all-to-all-done = bf16[2,64,1728]{2,0,1:T(2,128)(2,1)S(1)} async-done(((bf16[2,64,1728]{2,0,1:T(2,128)(2,1)}), bf16[2,64,1728]{2,0,1:T(2,128)(2,1)S(1)}, u32[]{:S(2)}, u32[]{:S(2)}) %all-to-all-start) | async-done | bytes 442400 | tf_op jit(solution)/shard_map/all_to_all | solution.py:125
  179.0 0.4 copy.65
  179.5 0.8 fusion.121
  180.2 1.9 reshape.123
  182.1 1.0 reshape.124
  183.1 1.2 reshape.122
  184.3 1.1 fusion.42
  185.4 2.2 fusion.128
  187.6 2.3 fusion.22
  189.9 1.0 copy.71
  190.9 0.9 convert_element_type.101
  191.8 0.9 copy.72
  192.7 0.8 copy.73
  193.5 5.9 all-to-all-start.1
  199.4 2.2 fusion.25
  201.6 1.0 copy.87
  202.6 0.9 concatenate.17
  203.5 1.9 fusion.24
  205.5 0.9 concatenate.16
  206.3 2.0 fusion.23
  208.4 0.9 concatenate.15
  209.3 1.2 concatenate.18
  210.6 1.2 copy.89
  211.8 8.0 %all-to-all-start.3 = ((bf16[64,2,1728]{2,1,0:T(2,128)(2,1)}), bf16[64,2,1728]{2,1,0:T(2,128)(2,1)}, u32[]{:S(2)}, u32[]{:S(2)}) async-start(bf16[64,2,1728]{2,1,0:T(2,128)(2,1)} %copy.89), calls=%async_computation.3 | async-start | bytes 917504 | tf_op jit(solution)/shard_map/all_to_all | solution.py:146
  219.8 1.7 copy.198
  221.5 1.0 reshape.126
  222.6 1.6 convolution_convert_fusion
  224.2 8.9 %all-to-all-done.3 = bf16[64,2,1728]{2,1,0:T(2,128)(2,1)} async-done(((bf16[64,2,1728]{2,1,0:T(2,128)(2,1)}), bf16[64,2,1728]{2,1,0:T(2,128)(2,1)}, u32[]{:S(2)}, u32[]{:S(2)}) %all-to-all-start.3) | async-done | bytes 442400 | tf_op jit(solution)/shard_map/all_to_all | solution.py:146
  233.1 2.1 copy.197
  235.2 2.2 reshape.132
  237.4 3.1 fusion.6
  240.5 1.6 convolution_convert_fusion.1
  242.2 1.3 dynamic-slice.2
  243.5 1.3 dynamic-slice
  246.1 1.1 fusion.8
  247.2 0.5 convolution_convert_fusion.12
  248.4 0.3 copy-done.16
  248.7 1.7 fusion.26
  250.4 0.4 fusion.28
  250.8 275.0 %all-reduce.9.cloned.1.call-done = (bf16[576,1152]{1,0:T(8,128)(2,1)}, bf16[576,1152]{1,0:T(8,128)(2,1)}) async-done(((bf16[576,1152]{1,0:T(8,128)(2,1)}, bf16[576,1152]{1,0:T(8,128)(2,1)}), (bf16[576,1152]{1,0:T(8,128)(2,1)}, bf16[576,1152]{1,0:T(8,128)(2,1)})) %all-reduce.9.cloned.1.call-update) | async-done | bytes 2654224
  525.8 1.6 constant_dynamic-slice_fusion
  527.4 1.6 fusion.27
  530.2 1.0 concatenate.19
  531.1 200.7 %all-reduce.11.cloned.1.call-done = (bf16[18,1152]{1,0:T(8,128)(2,1)}, bf16[18,1152]{1,0:T(8,128)(2,1)}) async-done(((bf16[18,1152]{1,0:T(8,128)(2,1)}, bf16[18,1152]{1,0:T(8,128)(2,1)}), (bf16[18,1152]{1,0:T(8,128)(2,1)}, bf16[18,1152]{1,0:T(8,128)(2,1)})) %all-reduce.11.cloned.1.call-update) | async-done | bytes 82960
  731.8 1.4 dynamic-slice_convert_fusion.1
  733.2 1.4 dynamic-slice_convert_fusion
  (58 shorter events, 3.5 us)
Async XLA Ops:
  7.2 1.3 copy-start
  7.2 142.2 %all-gather.3.cloned.1.call-start = ((), (), s32[]{:S(2)}) async-start(), calls=%async_computation.4 | async-start | bytes 4386816 | tf_op jit(solution)/shard_map/all_gather | solution.py:99
  8.5 12.6 %copy-start.11 = (bf16[2,64,1728]{2,1,0:T(8,128)(2,1)S(1)}, bf16[2,64,1728]{2,1,0:T(8,128)(2,1)}, u32[]{:S(2)}) copy-start(bf16[2,64,1728]{2,1,0:T(8,128)(2,1)} %param.7) | copy-start | bytes 1327108
  11.0 149.7 %all-to-all-start.2 = ((bf16[2,64,576]{2,0,1:T(2,128)(2,1)}), bf16[2,64,576]{2,0,1:T(2,128)(2,1)}, u32[]{:S(2)}, u32[]{:S(2)}) async-start(bf16[2,64,576]{2,0,1:T(2,128)(2,1)} %copy.76), calls=%async_computation.2 | async-start | bytes 327680 | tf_op jit(solution)/shard_map/all_to_all | solution.py:141
  21.5 1.8 copy-start.13
  21.8 1.5 copy-start.15
  22.1 1.2 copy-start.8
  23.3 3.7 copy-start.1
  23.3 3.7 copy-start.12
  27.0 127.2 %copy-start.4 = (bf16[128,576]{1,0:T(8,128)(2,1)}, bf16[128,576]{1,0:T(8,128)(2,1)S(1)}, u32[]{:S(2)}) copy-start(bf16[128,576]{1,0:T(8,128)(2,1)S(1)} %convert_element_type.94) | copy-start | bytes 442372
  160.8 18.3 %all-to-all-start = ((bf16[2,64,1728]{2,0,1:T(2,128)(2,1)}), bf16[2,64,1728]{2,0,1:T(2,128)(2,1)S(1)}, u32[]{:S(2)}, u32[]{:S(2)}) async-start(bf16[2,64,1728]{2,0,1:T(2,128)(2,1)} %copy.64), calls=%async_computation | async-start | bytes 917504 | tf_op jit(solution)/shard_map/all_to_all | solution.py:125
  179.5 4.9 copy-start.10
  193.5 18.3 %all-to-all-start.1 = ((bf16[64,2,576]{2,1,0:T(2,128)(2,1)}), bf16[64,2,576]{2,1,0:T(2,128)(2,1)}, u32[]{:S(2)}, u32[]{:S(2)}) async-start(bf16[64,2,576]{2,1,0:T(2,128)(2,1)} %copy.73), calls=%async_computation.1 | async-start | bytes 327680 | tf_op jit(solution)/shard_map/all_to_all | solution.py:128
  210.6 12.0 %copy-start.2 = (bf16[2,64,1152]{2,1,0:T(8,128)(2,1)S(1)}, bf16[2,64,1152]{2,1,0:T(8,128)(2,1)}, u32[]{:S(2)}) copy-start(bf16[2,64,1152]{2,1,0:T(8,128)(2,1)} %param.11) | copy-start | bytes 884740
  211.8 21.3 %all-to-all-start.3 = ((bf16[64,2,1728]{2,1,0:T(2,128)(2,1)}), bf16[64,2,1728]{2,1,0:T(2,128)(2,1)}, u32[]{:S(2)}, u32[]{:S(2)}) async-start(bf16[64,2,1728]{2,1,0:T(2,128)(2,1)} %copy.89), calls=%async_computation.3 | async-start | bytes 917504 | tf_op jit(solution)/shard_map/all_to_all | solution.py:146
  219.8 306.0 %all-reduce.9.cloned.1.call-start = ((), (), s32[]{:S(2)}) async-start(), calls=%async_computation.5 | async-start | bytes 5308416
  222.6 12.7 %copy-start.6 = (bf16[128,576]{1,0:T(8,128)(2,1)}, bf16[128,576]{1,0:T(8,128)(2,1)S(1)}, u32[]{:S(2)}) copy-start(bf16[128,576]{1,0:T(8,128)(2,1)S(1)} %reshape.126) | copy-start | bytes 442372
  237.4 3.1 copy-start.5
  240.5 6.7 copy-start.3
  242.1 3.9 copy-start.7
  242.2 489.6 %all-reduce.11.cloned.1.call-start = ((), (), s32[]{:S(2)}) async-start(), calls=%async_computation.6 | async-start | bytes 221184
  247.2 1.0 copy-start.9
  247.7 1.0 copy-start.16
  248.7 1.7 copy-start.14
Sparse Core Ops, SparseCore 0:
  11.1 138.2 all-gather.2
  242.3 283.4 all-reduce.8
  528.8 202.9 all-reduce.10
where the time goes:
time: 742 us; the launch traced here: 741 us
  waiting for transfers between devices  617 us (83%)
  local copies, waits for them, and re-layouts  43.8 us (6%)
  matrix products  33.1 us (4%)
  starting transfers between devices  29 us (4%)
  between operations  15.5 us (2%)
    unnamed x5, waiting for transfers between devices  476 us
    all_gather x1, waiting for transfers between devices, forward_project(): lax.all_gather(weight_shard, 'dp', axis=1, tiled=True)  122 us
  transfers between devices with their start and end apart: 7, of which 5 were waited for; matrix products, arithmetic and copies ran while one was open for 7% of the time, Pallas kernels for 0%

commit v1 on v0

--- a/solution.py
+++ b/solution.py
@@ -96,7 +96,9 @@
 def forward_project(hidden_rows, weight_shard):
     return jnp.dot(
         hidden_rows,
-        lax.all_gather(weight_shard, "dp", axis=1, tiled=True),
+        jnp.concatenate(
+            lax.all_to_all(jnp.stack([weight_shard] * lax.axis_size("dp")), "dp", 0, 0), axis=1
+        ),
         preferred_element_type=jnp.float32,
     )
 

time: 742 us -> 886 us (1.19)
  waiting for transfers between devices: 617 us -> 726 us
  starting transfers between devices: 29 us -> 47.9 us
  local copies, waits for them, and re-layouts: 43.8 us -> 58.7 us
    all_to_all x0 -> x1, waiting for transfers between devices: none -> 198 us  [forward_project(): lax.all_to_all(jnp.stack([weight_shard] * lax.axis_size('dp')), 'dp', 0, 0)]
    all_gather x1, waiting for transfers between devices: 122 us -> 0.02 us  [backward_project(): lax.all_gather(weight_shard, 'dp', axis=1, tiled=True)]
    all_to_all x1, waiting for transfers between devices: 9.68 us -> 42 us  [shards(): lax.all_to_all(frame_qkv, 'seq', split_axis=1, concat_axis=0, tiled=True)]
    all_to_all x0 -> x1, starting transfers between devices: none -> 18 us  [forward_project(): lax.all_to_all(jnp.stack([weight_shard] * lax.axis_size('dp')), 'dp', 0, 0)]
  transfers between devices with their start and end apart: 7 -> 8, of which waited for: 5 -> 5; matrix products, arithmetic and copies ran while one was open for 7% -> 9% of each run, Pallas kernels for 0% -> 0%
where the time goes in v1:
time: 886 us; the launch traced here: 884 us
  waiting for transfers between devices  726 us (82%)
  local copies, waits for them, and re-layouts  58.7 us (7%)
  starting transfers between devices  47.9 us (5%)
  matrix products  33.4 us (4%)
  between operations  15.4 us (2%)
    unnamed x5, waiting for transfers between devices  483 us
    all_to_all x1, waiting for transfers between devices, forward_project(): lax.all_to_all(jnp.stack([weight_shard] * lax.axis_size('dp')), 'dp', 0, 0)  198 us
    all_to_all x1, waiting for transfers between devices, shards(): lax.all_to_all(frame_qkv, 'seq', split_axis=1, concat_axis=0, tiled=True)  42 us
    all_to_all x1, starting transfers between devices, forward_project(): lax.all_to_all(jnp.stack([weight_shard] * lax.axis_size('dp')), 'dp', 0, 0)  18 us
  transfers between devices with their start and end apart: 8, of which 5 were waited for; matrix products, arithmetic and copies ran while one was open for 9% of the time, Pallas kernels for 0%

profile of v1, /device:TPU:2, one launch (start us, length us, event | category | flops | bytes accessed | tf_op | source)
XLA Modules:
  0.0 884.5 jit_solution(16105180142501121069)
XLA Ops:
  7.2 3.4 stack.2
  10.6 18.0 %all-to-all-start = ((bf16[16,1152,108]{1,2,0:T(8,128)(2,1)}), bf16[16,1152,108]{1,2,0:T(8,128)(2,1)}, u32[]{:S(2)}, u32[]{:S(2)}) async-start(bf16[16,1152,108]{1,2,0:T(8,128)(2,1)} %stack.2), calls=%async_computation | async-start | bytes 8257536 | tf_op jit(solution)/shard_map/all_to_all | solution.py:100
  28.7 0.7 all-gather.3.cloned.1.call-update
  30.3 1.1 fusion.123
  32.4 0.5 convolution_convert_fusion.13
  33.1 0.8 copy.77
  33.9 197.8 %all-to-all-done = bf16[16,1152,108]{1,2,0:T(8,128)(2,1)} async-done(((bf16[16,1152,108]{1,2,0:T(8,128)(2,1)}), bf16[16,1152,108]{1,2,0:T(8,128)(2,1)}, u32[]{:S(2)}, u32[]{:S(2)}) %all-to-all-start) | async-done | bytes 3981344 | tf_op jit(solution)/shard_map/all_to_all | solution.py:100
  231.8 7.2 all-to-all-start.3
  238.9 1.4 fusion.7
  240.3 5.1 reshape.128
  245.4 4.1 convolution_convert_fusion.3
  249.5 2.0 copy.64
  251.5 2.3 copy.65
  253.8 7.9 all-to-all-start.1
  261.7 1.0 copy.78
  262.7 0.7 copy.79
  263.4 1.9 reshape_reshape.6
  265.3 42.0 %all-to-all-done.1 = bf16[2,64,1728]{2,0,1:T(2,128)(2,1)} async-done(((bf16[2,64,1728]{2,0,1:T(2,128)(2,1)}), bf16[2,64,1728]{2,0,1:T(2,128)(2,1)}, u32[]{:S(2)}, u32[]{:S(2)}) %all-to-all-start.1) | async-done | bytes 442400 | tf_op jit(solution)/shard_map/all_to_all | solution.py:127
  307.3 1.4 copy.66
  308.7 0.8 fusion.121
  309.5 1.2 reshape.132
  310.7 2.0 reshape.134
  312.7 1.9 reshape.133
  314.6 2.2 fusion.128
  316.9 2.3 fusion.22
  319.1 1.0 copy.72
  320.1 0.9 convert_element_type.101
  321.0 0.9 copy.73
  321.9 0.8 copy.74
  322.8 6.9 all-to-all-start.2
  329.7 2.1 fusion.42
  331.8 2.6 fusion.23
  334.4 1.0 copy.84
  335.4 0.9 concatenate.15
  336.3 2.6 fusion.24
  338.9 1.0 copy.86
  339.9 0.9 concatenate.16
  340.8 2.3 fusion.25
  343.1 1.0 copy.88
  344.1 0.9 concatenate.17
  345.0 2.0 concatenate.18
  347.0 1.0 copy.89
  348.0 1.2 copy.90
  349.3 7.8 all-to-all-start.4
  357.1 4.9 reshape.149
  362.1 1.7 copy.199
  363.7 1.0 reshape.136
  364.8 1.6 convolution_convert_fusion
  366.4 4.0 all-to-all-done.4
  370.4 2.1 copy.198
  372.5 2.1 reshape.142
  374.6 3.1 fusion.6
  377.7 1.7 convolution_convert_fusion.1
  379.5 1.3 dynamic-slice
  380.7 1.3 dynamic-slice.2
  383.3 1.1 fusion.8
  386.1 1.6 fusion.26
  388.1 281.1 %all-reduce.9.cloned.1.call-done = (bf16[576,1152]{1,0:T(8,128)(2,1)}, bf16[576,1152]{1,0:T(8,128)(2,1)}) async-done(((bf16[576,1152]{1,0:T(8,128)(2,1)}, bf16[576,1152]{1,0:T(8,128)(2,1)}), (bf16[576,1152]{1,0:T(8,128)(2,1)}, bf16[576,1152]{1,0:T(8,128)(2,1)})) %all-reduce.9.cloned.1.call-update) | async-done | bytes 2654224
  669.2 1.6 constant_dynamic-slice_fusion
  670.8 1.5 fusion.27
  673.5 1.0 concatenate.19
  674.4 200.8 %all-reduce.11.cloned.1.call-done = (bf16[18,1152]{1,0:T(8,128)(2,1)}, bf16[18,1152]{1,0:T(8,128)(2,1)}) async-done(((bf16[18,1152]{1,0:T(8,128)(2,1)}, bf16[18,1152]{1,0:T(8,128)(2,1)}), (bf16[18,1152]{1,0:T(8,128)(2,1)}, bf16[18,1152]{1,0:T(8,128)(2,1)})) %all-reduce.11.cloned.1.call-update) | async-done | bytes 82960
  875.2 1.4 dynamic-slice_convert_fusion.1
  876.6 1.4 dynamic-slice_convert_fusion
  (62 shorter events, 5.4 us)
Async XLA Ops:
  7.2 25.2 %copy-start = (bf16[576,1152]{1,0:T(8,128)(2,1)S(1)}, bf16[576,1152]{1,0:T(8,128)(2,1)}, u32[]{:S(2)}) copy-start(bf16[576,1152]{1,0:T(8,128)(2,1)} %param.10) | copy-start | bytes 3981316
  10.6 18.8 %copy-start.11 = (bf16[2,64,1728]{2,1,0:T(8,128)(2,1)S(1)}, bf16[2,64,1728]{2,1,0:T(8,128)(2,1)}, u32[]{:S(2)}) copy-start(bf16[2,64,1728]{2,1,0:T(8,128)(2,1)} %param.7) | copy-start | bytes 1327108
  10.6 221.2 %all-to-all-start = ((bf16[16,1152,108]{1,2,0:T(8,128)(2,1)}), bf16[16,1152,108]{1,2,0:T(8,128)(2,1)}, u32[]{:S(2)}, u32[]{:S(2)}) async-start(bf16[16,1152,108]{1,2,0:T(8,128)(2,1)} %stack.2), calls=%async_computation | async-start | bytes 8257536 | tf_op jit(solution)/shard_map/all_to_all | solution.py:100
  28.6 328.5 %all-gather.3.cloned.1.call-start = ((), (), s32[]{:S(2)}) async-start(), calls=%async_computation.5 | async-start | bytes 4386816 | tf_op jit(solution)/shard_map/all_gather | solution.py:107
  29.8 1.7 copy-start.8
  30.0 1.9 copy-start.14
  30.3 1.6 copy-start.12
  31.5 1.0 copy-start.2
  32.4 206.6 %copy-start.4 = (bf16[128,576]{1,0:T(8,128)(2,1)}, bf16[128,576]{1,0:T(8,128)(2,1)S(1)}, u32[]{:S(2)}) copy-start(bf16[128,576]{1,0:T(8,128)(2,1)S(1)} %convert_element_type.94) | copy-start | bytes 442372
  32.4 206.5 %copy-start.1 = (bf16[576,1152]{1,0:T(8,128)(2,1)S(1)}, bf16[576,1152]{1,0:T(8,128)(2,1)}, u32[]{:S(2)}) copy-start(bf16[576,1152]{1,0:T(8,128)(2,1)} %param.8) | copy-start | bytes 3981316
  231.8 22.0 %all-to-all-start.3 = ((bf16[2,64,576]{2,0,1:T(2,128)(2,1)}), bf16[2,64,576]{2,0,1:T(2,128)(2,1)}, u32[]{:S(2)}, u32[]{:S(2)}) async-start(bf16[2,64,576]{2,0,1:T(2,128)(2,1)} %copy.77), calls=%async_computation.3 | async-start | bytes 327680 | tf_op jit(solution)/shard_map/all_to_all | solution.py:143
  253.8 53.5 %all-to-all-start.1 = ((bf16[2,64,1728]{2,0,1:T(2,128)(2,1)}), bf16[2,64,1728]{2,0,1:T(2,128)(2,1)}, u32[]{:S(2)}, u32[]{:S(2)}) async-start(bf16[2,64,1728]{2,0,1:T(2,128)(2,1)} %copy.65), calls=%async_computation.1 | async-start | bytes 917504 | tf_op jit(solution)/shard_map/all_to_all | solution.py:127
  310.7 6.1 copy-start.10
  322.8 9.0 %copy-start.16 = (bf16[8,16,8,72]{3,2,1,0:T(8,128)(2,1)S(1)}, bf16[8,16,8,72]{3,2,1,0:T(8,128)(2,1)}, u32[]{:S(2)}) copy-start(bf16[8,16,8,72]{3,2,1,0:T(8,128)(2,1)} %reshape.134) | copy-start | bytes 442372
  322.8 26.5 %all-to-all-start.2 = ((bf16[64,2,576]{2,1,0:T(2,128)(2,1)}), bf16[64,2,576]{2,1,0:T(2,128)(2,1)}, u32[]{:S(2)}, u32[]{:S(2)}) async-start(bf16[64,2,576]{2,1,0:T(2,128)(2,1)} %copy.74), calls=%async_computation.2 | async-start | bytes 327680 | tf_op jit(solution)/shard_map/all_to_all | solution.py:130
  349.3 21.1 %all-to-all-start.4 = ((bf16[64,2,1728]{2,1,0:T(2,128)(2,1)}), bf16[64,2,1728]{2,1,0:T(2,128)(2,1)}, u32[]{:S(2)}, u32[]{:S(2)}) async-start(bf16[64,2,1728]{2,1,0:T(2,128)(2,1)} %copy.90), calls=%async_computation.4 | async-start | bytes 917504 | tf_op jit(solution)/shard_map/all_to_all | solution.py:148
  357.0 312.1 %all-reduce.9.cloned.1.call-start = ((), (), s32[]{:S(2)}) async-start(), calls=%async_computation.6 | async-start | bytes 5308416
  364.8 7.7 copy-start.6
  374.6 3.1 copy-start.5
  377.7 6.7 copy-start.3
  379.4 3.9 copy-start.7
  379.4 495.8 %all-reduce.11.cloned.1.call-start = ((), (), s32[]{:S(2)}) async-start(), calls=%async_computation.7 | async-start | bytes 221184
  384.4 1.0 copy-start.9
  385.1 1.0 copy-start.15
  386.1 1.6 copy-start.13
Sparse Core Ops, SparseCore 0:
  32.5 273.7 all-gather.2
  379.5 289.5 all-reduce.8
  672.2 202.9 all-reduce.10
